TPU v7x, 32 devices: a whole 2x2x4 slice. The times are simulated.
32 devices in a mesh: dp: 4 (over y, x), shard: 8 (over z, core).
Axes of the slice: x: 2, y: 2, z: 4, core: 2. Of those that a mesh axis runs over, the one named last changes fastest.
Arguments:
- id_table: float32 [262144, 128], P(('dp', 'shard')), may hold values from -6 to 6
- ada_state: float32 [262144], P(('dp', 'shard')), may hold values from 0.01 to 1
- user_first: float32 [128, 512], replicated, may hold values from -0.5 to 0.5
- user_second: float32 [512, 128], replicated, may hold values from -0.25 to 0.25
- item_first: float32 [128, 512], replicated, may hold values from -0.5 to 0.5
- item_second: float32 [512, 128], replicated, may hold values from -0.25 to 0.25
- fetch_rows: int32 [32, 4, 8, 72], P(('dp', 'shard')), may hold values from 0 to 8191
- lookup_slots: int32 [32, 1536], P(('dp', 'shard')), may hold values from 0 to 2303
Outputs:
- new_table: float32 [262144, 128], P(('dp', 'shard'))
- new_state: float32 [262144], P(('dp', 'shard'))
- user_first_grad: float32 [128, 512], replicated
- user_second_grad: float32 [512, 128], replicated
- item_first_grad: float32 [128, 512], replicated
- item_second_grad: float32 [512, 128], replicated
- mean_loss: float32 [], replicated
All inputs are finite; a program needn't handle non-finite values.
Results may differ from a plain program's by a relative error of at most 0.0038.
The roundings to bfloat16 on the way count: a program that leaves them out, or rounds other values in their place, can miss the bound.
Values may be sent and summed in bfloat16 or wider, within the bound.
No kernel may reach another device: no remote copies, remote signals or barrier semaphores. Data moves between devices by JAX's collectives and lax.ppermute only.
A program may use at most 128 MiB of HBM per device.

v0:
```python
import jax
import jax.numpy as jnp
from jax import lax
from jax.sharding import PartitionSpec as P

EXAMPLES_ON_CHIP = 512
highest = lax.Precision.HIGHEST
logit_divisor = 0.025
learn_rate = 0.1
epsilon = 1e-08


def tower_pass(looked, first_w, second_w):
    hidden_act = jax.nn.silu(
        jnp.dot(looked, first_w, precision=highest, preferred_element_type=jnp.float32)
    )
    tower_out = jnp.dot(hidden_act, second_w, precision=highest, preferred_element_type=jnp.float32)
    return tower_out / jnp.sqrt(jnp.sum(tower_out * tower_out, axis=1, keepdims=True) + 1e-06)


def score_block(user_half_precision, candidate_half_precision):
    return (
        jnp.dot(user_half_precision, candidate_half_precision.T, preferred_element_type=jnp.float32)
        / logit_divisor
    )


def cand_step(candidate_half_precision, user_half_precision):
    exponent = jnp.exp(score_block(user_half_precision, candidate_half_precision))
    collected_entries = jnp.dot(
        exponent.astype(jnp.bfloat16), candidate_half_precision, preferred_element_type=jnp.float32
    )
    return (jnp.sum(exponent, axis=1), collected_entries)


def item_term(user_half_precision, log_z, candidate_half_precision):
    softmax = jnp.exp(
        score_block(user_half_precision, candidate_half_precision) - log_z[:, None]
    ).astype(jnp.bfloat16)
    return jnp.dot(softmax.T, user_half_precision, preferred_element_type=jnp.float32)


def per_device(
    id_table, ada_state, user_first, user_second, item_first, item_second, fetch_rows, lookup_slots
):
    target_index_vector = id_table.shape[1]
    examples_on_chip = EXAMPLES_ON_CHIP
    asked_rows = lax.all_to_all(
        lax.all_to_all(fetch_rows[0], "dp", split_axis=0, concat_axis=0, tiled=True),
        "shard",
        split_axis=1,
        concat_axis=1,
        tiled=True,
    )
    fetched = jnp.take(id_table, asked_rows.reshape(-1), axis=0).reshape(
        asked_rows.shape + (target_index_vector,)
    )
    returned = lax.all_to_all(
        lax.all_to_all(fetched, "dp", split_axis=0, concat_axis=0, tiled=True),
        "shard",
        split_axis=1,
        concat_axis=1,
        tiled=True,
    )
    slot_rows = returned.reshape(-1, target_index_vector)
    slot_index = lookup_slots[0]
    looked = jnp.take(slot_rows, slot_index, axis=0)
    user_vec, user_pull = jax.vjp(tower_pass, looked[:examples_on_chip], user_first, user_second)
    item_vec, item_pull = jax.vjp(tower_pass, looked[examples_on_chip:], item_first, item_second)
    user_half_precision = user_vec.astype(jnp.bfloat16)
    item_bf = item_vec.astype(jnp.bfloat16)
    query_single_float = user_half_precision.astype(jnp.float32)
    resident_target_entries = item_bf[:examples_on_chip].astype(jnp.float32)
    matching_pair_logit = (
        jnp.sum(query_single_float * resident_target_entries, axis=1) / logit_divisor
    )
    reduced_aggregates, collected_entries = cand_step(
        lax.all_gather(item_bf, "dp", axis=0, tiled=True), user_half_precision
    )
    log_z = jnp.log(reduced_aggregates)
    target_derivative_accrual = item_term(
        lax.all_gather(user_vec, "dp", axis=0, tiled=True).astype(jnp.bfloat16),
        lax.all_gather(log_z, "dp", axis=0, tiled=True),
        item_bf,
    )
    query_adjoint = (
        collected_entries / reduced_aggregates[:, None] - resident_target_entries
    ) / logit_divisor
    target_adjoint = (
        target_derivative_accrual.at[:examples_on_chip].add(-query_single_float) / logit_divisor
    )
    user_look, user_first_g, user_second_g = user_pull(query_adjoint)
    item_look, item_first_g, item_second_g = item_pull(target_adjoint)
    look_grads = jnp.concatenate([user_look, item_look], axis=0)
    slot_grads = jnp.zeros_like(slot_rows).at[slot_index].add(look_grads)
    sent_back = lax.all_to_all(
        lax.all_to_all(
            slot_grads.reshape(returned.shape).astype(jnp.bfloat16),
            "dp",
            split_axis=0,
            concat_axis=0,
            tiled=True,
        ),
        "shard",
        split_axis=1,
        concat_axis=1,
        tiled=True,
    ).astype(jnp.float32)
    grad_rows = (
        jnp.zeros_like(id_table)
        .at[asked_rows.reshape(-1)]
        .add(sent_back.reshape(-1, target_index_vector))
    )
    new_state = ada_state + jnp.mean(grad_rows * grad_rows, axis=1)
    new_table = id_table - learn_rate * grad_rows / (jnp.sqrt(new_state)[:, None] + epsilon)
    loss_part = jnp.sum(log_z - matching_pair_logit)
    summed = lax.psum(
        (user_first_g, user_second_g, item_first_g, item_second_g, loss_part), ("dp", "shard")
    )
    shard_number = lax.axis_size("dp") * lax.axis_size("shard")
    return (
        new_table,
        new_state,
        summed[0] / shard_number,
        summed[1] / shard_number,
        summed[2] / shard_number,
        summed[3] / shard_number,
        summed[4] / (shard_number * examples_on_chip),
    )


def solution(mesh):
    return jax.shard_map(
        per_device,
        mesh=mesh,
        in_specs=(
            P(("dp", "shard"), None),
            P(("dp", "shard")),
            P(),
            P(),
            P(),
            P(),
            P(("dp", "shard"), None, None, None),
            P(("dp", "shard"), None),
        ),
        out_specs=(P(("dp", "shard"), None), P(("dp", "shard")), P(), P(), P(), P(), P()),
        check_vma=False,
    )
```

profile of v0, /device:TPU:0, one launch (start us, length us, event | category | flops | bytes accessed | tf_op | source)
XLA Modules:
  0.0 361.9 jit_solution(15782953325688524731)
XLA Ops:
  7.2 10.0 %all_to_all.30 = s32[4,8,72]{2,1,0:T(8,128)S(1)} all-to-all(s32[4,8,72]{2,1,0:T(8,128)} %bitcast.34), channel_id=1, replica_groups=mesh['dp'=4,'shard'=8] {'dp'}, dimensions={0} | all-to-all | bytes 18432 | tf_op jit(solution)/shard_map/all_to_all | solution.py:49
  17.2 10.3 %all_to_all.31 = s32[4,8,72]{2,0,1:T(4,128)S(1)} all-to-all(s32[4,8,72]{2,0,1:T(4,128)S(1)} %copy.24), channel_id=1, replica_groups=mesh['dp'=4,'shard'=8] {'shard'}, dimensions={1} | all-to-all | bytes 18432 | tf_op jit(solution)/shard_map/all_to_all | solution.py:48
  27.7 0.6 copy-done.14
  28.3 6.1 %gather_fusion = f32[2304,128]{1,0:T(8,128)S(1)} fusion(f32[8192,128]{1,0:T(8,128)} %param.10, s32[3072]{0:T(1024)S(1)} %pad_clamp_fusion), kind=kCustom, calls=%fused_computation | custom fusion | bytes 2368512 | tf_op jit(solution)/shard_map/jit(_take)/gather | solution.py:55
  34.9 18.2 %all_to_all.32 = f32[4,8,72,128]{3,2,1,0:T(8,128)S(1)} all-to-all(f32[4,8,72,128]{3,2,1,0:T(8,128)S(1)} %broadcast_select_fusion), channel_id=1, replica_groups=mesh['dp'=4,'shard'=8] {'dp'}, dimensions={0} | all-to-all | bytes 2359296 | tf_op jit(solution)/shard_map/all_to_all | solution.py:59
  53.1 1.1 copy.27
  54.2 3.6 all-to-all-start.3
  57.9 29.1 %all-to-all-done.3 = f32[4,8,72,128]{3,2,0,1:T(8,128)S(1)} async-done(((f32[4,8,72,128]{3,2,0,1:T(8,128)}), f32[4,8,72,128]{3,2,0,1:T(8,128)S(1)}, u32[]{:S(2)}, u32[]{:S(2)}) %all-to-all-start.3) | async-done | bytes 1179680 | tf_op jit(solution)/shard_map/all_to_all | solution.py:58
  87.2 2.6 gather_fusion.1
  90.1 1.8 fusion.30
  91.9 2.7 multiply_reduce_fusion.2
  94.7 0.7 divide_multiply_fusion
  95.5 0.8 divide_convert_fusion
  96.2 1.0 fusion.41
  97.3 2.7 multiply_reduce_fusion.4
  100.7 0.6 fusion.38
  101.3 11.5 %all_gather.10 = bf16[2048,128]{0,1:T(8,128)(2,1)} all-gather(bf16[512,128]{0,1:T(8,128)(2,1)S(1)} %get-tuple-element.24), channel_id=1, replica_groups=mesh['dp'=4,'shard'=8] {'dp'}, dimensions={0}, use_global_device_ids=true | all-gather | bytes 655360 | tf_op jit(solution)/shard_map/all_gather | solution.py:82
  112.8 8.4 %all-gather.3.cloned.1.call-done = bf16[4096,128]{0,1:T(8,128)(2,1)} async-done(((bf16[1024,128]{0,1:T(8,128)(2,1)}), bf16[4096,128]{0,1:T(8,128)(2,1)}) %all-gather.3.cloned.1.call-update) | async-done | bytes 1048592 | tf_op jit(solution)/shard_map/all_gather | solution.py:78
  121.2 5.8 %fusion = (f32[512]{0:T(512)S(1)}, f32[512,4096]{1,0:T(8,128)}) fusion(bf16[512,128]{0,1:T(8,128)(2,1)S(1)} %get-tuple-element.24, bf16[4096,128]{0,1:T(8,128)(2,1)} %all-gather.3.cloned.1.call-done), kind=kOutput, calls=%fused_computation.6 | convolution fusion | flops 541064704 | bytes 9570304 | tf_op jit(solution)/shard_map/dot_general | solution.py:23
  127.0 0.6 subtract_reduce_fusion
  127.6 8.8 %all-gather = f32[4,1,512]{2,1,0:T(1,128)} all-gather(f32[1,1,512]{2,1,0:T(1,128)S(1)} %bitcast.36), channel_id=1, replica_groups=mesh['dp'=4,'shard'=8] {'dp'}, dimensions={0}, use_global_device_ids=true | all-gather | bytes 10240 | tf_op jit(solution)/shard_map/all_gather | solution.py:83
  136.5 4.1 %fusion.10 = f32[1024,128]{0,1:T(8,128)} fusion(bf16[1024,128]{0,1:T(8,128)(2,1)S(1)} %copy-done.3, f32[2048]{0:T(1024)} %bitcast.35, bf16[2048,128]{0,1:T(8,128)(2,1)} %all_gather.10), kind=kOutput, calls=%fused_computation.19 | convolution fusion | flops 1080033280 | bytes 1318912 | tf_op jit(solution)/shard_map/dot_general | solution.py:40
  140.6 1.7 fusion.37
  142.3 1.4 multiply_reduce_fusion.1
  143.7 0.8 multiply_multiply_fusion
  144.6 3.8 %fusion.6 = f32[1024,512]{1,0:T(8,128)S(1)} fusion(f32[1024,512]{1,0:T(8,128)S(1)} %fusion.30, f32[512,128]{1,0:T(8,128)S(1)} %copy-done, f32[1024,128]{0,1:T(8,128)} %copy-done.5, f32[1024,128]{0,1:T(8,128)} %fusion.37, f32[1024]{0:T(1024)S(1)} %multiply_multiply_fusion, f32[1024]{0:T(1024)} %copy-done.17), kind=kOutput, calls=%fused_computation.14 | convolution fusion | flops 810680320 | bytes 5513216 | tf_op jit(solution)/shard_map/transpose(jvp())/dot_general | solution.py:17
  148.4 2.1 fusion.28
  150.5 2.6 fusion.58
  153.1 1.6 multiply_reduce_fusion.3
  154.8 2.6 fusion.43
  157.4 1.6 fusion.19
  159.0 1.0 fusion.57
  160.0 9.3 %scatter_custom_fusion = f32[2304,128]{1,0:T(8,128)S(1)} fusion(s32[1536]{0:T(1024)S(1)} %fusion.48, f32[1024,128]{1,0:T(8,128)} %fusion.58, f32[]{:T(128)} %constant.111, f32[512,128]{1,0:T(8,128)S(1)} %fusion.57, f32[]{:T(128)} %constant.90.clone.1), kind=kCustom, calls=%fused_computation.28 | custom fusion | flops 393216 | bytes 1966088 | tf_op jit(solution)/shard_map/scatter-add | solution.py:95
  169.4 0.9 convert_element_type.35
  170.2 3.5 all-to-all-start.4
  173.7 6.2 %fusion.32 = f32[512,128]{1,0:T(8,128)} fusion(f32[1024,512]{1,0:T(8,128)} %copy-done.4, f32[1024,128]{0,1:T(8,128)} %copy-done.5, f32[1024,128]{0,1:T(8,128)} %fusion.37, f32[1024]{0:T(1024)S(1)} %copy-done.26, f32[1024]{0:T(1024)S(1)} %copy-done.18), kind=kOutput, calls=%fused_computation.45 | convolution fusion | flops 808058880 | bytes 3416064 | tf_op jit(solution)/shard_map/transpose(jvp())/dot_general | solution.py:17
  179.9 0.7 all-to-all-done.4
  180.7 0.9 copy.29
  181.5 4.6 %all-to-all-start.5 = ((bf16[4,8,72,128]{3,2,0,1:T(8,128)(2,1)}), bf16[4,8,72,128]{3,2,0,1:T(8,128)(2,1)S(1)}, u32[]{:S(2)}, u32[]{:S(2)}) async-start(bf16[4,8,72,128]{3,2,0,1:T(8,128)(2,1)} %copy.29), calls=%async_computation.5 | async-start | bytes 1179648 | tf_op jit(solution)/shard_map/all_to_all | solution.py:96
  186.2 1.5 fusion.39
  187.7 40.8 %psum.39 = f32[]{:T(128)} all-reduce(f32[]{:T(128)} %get-tuple-element.29), channel_id=1, replica_groups=mesh['dp'=4,'shard'=8] {'dp','shard'}, use_global_device_ids=true, to_apply=%region_14.15 | all-reduce | flops 1 | bytes 8 | tf_op jit(solution)/shard_map/psum | solution.py:117
  229.1 96.8 %all-reduce.3.cloned.1.call-done = (f32[128,512]{1,0:T(8,128)}, f32[512,128]{1,0:T(8,128)}, f32[128,512]{1,0:T(8,128)}, f32[512,128]{1,0:T(8,128)}) async-done(((f32[128,512]{1,0:T(8,128)}, f32[512,128]{1,0:T(8,128)}, f32[128,512]{1,0:T(8,128)}, f32[512,128]{1,0:T(8,128)}), (f32[128,512]{1,0:T(8,128)}, f32[512,128]{1,0:T(8,128)}, f32[128,512]{1,0:T(8,128)}, ...) | async-done | bytes 1048592 | tf_op jit(solution)/shard_map/psum | solution.py:117
  326.0 1.9 broadcast_multiply_fusion.2
  327.8 1.9 broadcast_multiply_fusion
  329.8 15.8 %scatter_custom_fusion.1 = f32[8192,128]{1,0:T(8,128)} fusion(s32[2304]{0:T(1024)} %copy-done.14, f32[]{:T(128)} %constant.90.clone.1, bf16[2304,128]{1,0:T(8,128)(2,1)S(1)} %bitcast.32), kind=kCustom, calls=%fused_computation.17 | custom fusion | flops 589824 | bytes 4784640 | tf_op jit(solution)/shard_map/scatter-add | solution.py:112
  345.6 3.5 multiply_reduce_fusion
  349.1 0.6 sqrt_add_fusion
  349.7 4.2 %divide_subtract_fusion = f32[8192,128]{1,0:T(8,128)} fusion(f32[8192,128]{1,0:T(8,128)S(1)} %copy-done.1, f32[8192,128]{1,0:T(8,128)} %scatter_custom_fusion.1, f32[8192]{0:T(1024)S(1)} %get-tuple-element.25), kind=kLoop, calls=%fused_computation.9 | loop fusion | flops 3145728 | bytes 12615680 | tf_op jit(solution)/shard_map/sub | solution.py:115
  (82 shorter events, 2.1 us)
Async XLA Ops:
  7.2 84.7 %copy-start = (f32[512,128]{1,0:T(8,128)S(1)}, f32[512,128]{1,0:T(8,128)}, u32[]{:S(2)}) copy-start(f32[512,128]{1,0:T(8,128)} %param.15) | copy-start | bytes 786436
  27.7 0.6 copy-start.14
  53.1 4.7 %copy-start.16 = (s32[1,1536]{1,0:T(1,128)S(1)}, s32[1,1536]{1,0:T(1,128)}, u32[]{:S(2)}) copy-start(s32[1,1536]{1,0:T(1,128)} %param.17) | copy-start | bytes 18436
  54.2 32.9 %all-to-all-start.3 = ((f32[4,8,72,128]{3,2,0,1:T(8,128)}), f32[4,8,72,128]{3,2,0,1:T(8,128)S(1)}, u32[]{:S(2)}, u32[]{:S(2)}) async-start(f32[4,8,72,128]{3,2,0,1:T(8,128)} %copy.27), calls=%async_computation.3 | async-start | bytes 2359296 | tf_op jit(solution)/shard_map/all_to_all | solution.py:58
  57.8 63.4 %all-gather.3.cloned.1.call-start = ((), (), s32[]{:S(2)}) async-start(), calls=%async_computation.6 | async-start | bytes 1310720 | tf_op jit(solution)/shard_map/all_gather | solution.py:78
  87.2 2.9 copy-start.12
  91.9 52.7 %copy-start.4 = (f32[1024,512]{1,0:T(8,128)}, f32[1024,512]{1,0:T(8,128)S(1)}, u32[]{:S(2)}) copy-start(f32[1024,512]{1,0:T(8,128)S(1)} %fusion.30) | copy-start | bytes 6291460
  91.9 4.3 %copy-start.10 = (f32[128,512]{1,0:T(8,128)S(1)}, f32[128,512]{1,0:T(8,128)}, u32[]{:S(2)}) copy-start(f32[128,512]{1,0:T(8,128)} %param.12) | copy-start | bytes 786436
  94.7 0.8 copy-start.5
  94.7 5.3 %copy-start.19 = (f32[1024]{0:T(1024)}, f32[1024]{0:T(1024)S(1)}, u32[]{:S(2)}) copy-start(f32[1024]{0:T(1024)S(1)} %get-tuple-element.33) | copy-start | bytes 12292
  95.4 4.6 %copy-start.17 = (f32[1024]{0:T(1024)}, f32[1024]{0:T(1024)S(1)}, u32[]{:S(2)}) copy-start(f32[1024]{0:T(1024)S(1)} %get-tuple-element.28) | copy-start | bytes 12292
  97.2 2.7 copy-start.8
  97.2 3.4 copy-start.3
  99.9 0.6 copy-start.23
  100.0 0.7 copy-start.6
  100.0 12.9 %copy-start.20 = (f32[512]{0:T(512)}, f32[512]{0:T(512)S(1)}, u32[]{:S(2)}) copy-start(f32[512]{0:T(512)S(1)} %get-tuple-element.32) | copy-start | bytes 6148
  121.2 5.8 %copy-start.22 = (f32[512]{0:T(512)S(1)}, f32[512]{0:T(512)}, u32[]{:S(2)}) copy-start(f32[512]{0:T(512)} %get-tuple-element.23) | copy-start | bytes 6148
  142.3 10.8 %slice-start = ((s8[8388608]{0:T(1024)(128)(4,1)}), s8[4194304]{0:T(1024)(128)(4,1)S(1)}, s32[]{:S(2)}) async-start(s8[8388608]{0:T(1024)(128)(4,1)} %bitcast.28), calls=%async_computation.8 | async-start | bytes 8388608
  144.6 3.8 %copy-start.25 = (f32[1024]{0:T(1024)}, f32[1024]{0:T(1024)S(1)}, u32[]{:S(2)}) copy-start(f32[1024]{0:T(1024)S(1)} %multiply_multiply_fusion) | copy-start | bytes 12292
  144.6 8.5 %slice-start.1 = ((s8[8388608]{0:T(1024)(128)(4,1)}), s8[4194304]{0:T(1024)(128)(4,1)S(1)}, s32[]{:S(2)}) async-start(s8[8388608]{0:T(1024)(128)(4,1)} %bitcast.28), calls=%async_computation.9 | async-start | bytes 8388608
  148.4 2.1 copy-start.13
  150.5 2.6 copy-start.2
  150.5 2.6 copy-start.7
  153.1 1.6 copy-start.24
  153.1 1.6 copy-start.9
  153.1 1.6 copy-start.21
  154.8 2.6 copy-start.27
  157.4 1.6 copy-start.11
  160.0 13.7 %copy-start.18 = (f32[1024]{0:T(1024)S(1)}, f32[1024]{0:T(1024)}, u32[]{:S(2)}) copy-start(f32[1024]{0:T(1024)} %copy-done.17) | copy-start | bytes 12292
  160.0 13.7 %copy-start.26 = (f32[1024]{0:T(1024)S(1)}, f32[1024]{0:T(1024)}, u32[]{:S(2)}) copy-start(f32[1024]{0:T(1024)} %copy-done.25) | copy-start | bytes 12292
  170.2 10.4 %all-to-all-start.4 = ((bf16[4,8,72,128]{3,2,1,0:T(8,128)(2,1)}), bf16[4,8,72,128]{3,2,1,0:T(8,128)(2,1)S(1)}, u32[]{:S(2)}, u32[]{:S(2)}) async-start(bf16[4,8,72,128]{3,2,1,0:T(8,128)(2,1)} %bitcast.33), calls=%async_computation.4 | async-start | bytes 1179648 | tf_op jit(solution)/shard_map/all_to_all | solution.py:97
  181.5 148.2 %all-to-all-start.5 = ((bf16[4,8,72,128]{3,2,0,1:T(8,128)(2,1)}), bf16[4,8,72,128]{3,2,0,1:T(8,128)(2,1)S(1)}, u32[]{:S(2)}, u32[]{:S(2)}) async-start(bf16[4,8,72,128]{3,2,0,1:T(8,128)(2,1)} %copy.29), calls=%async_computation.5 | async-start | bytes 1179648 | tf_op jit(solution)/shard_map/all_to_all | solution.py:96
  186.1 139.9 %all-reduce.3.cloned.1.call-start = ((), (), s32[]{:S(2)}) async-start(), calls=%async_computation.7 | async-start | bytes 2097152 | tf_op jit(solution)/shard_map/psum | solution.py:117
  345.6 3.5 copy-start.15
  345.6 4.1 %copy-start.1 = (f32[8192,128]{1,0:T(8,128)S(1)}, f32[8192,128]{1,0:T(8,128)}, u32[]{:S(2)}) copy-start(f32[8192,128]{1,0:T(8,128)} %param.10) | copy-start | bytes 12582916
Sparse Core Ops, SparseCore 0:
  96.4 24.8 all-gather.2
  193.0 132.9 all-reduce.2
where the time goes:
time: 363 us; the launch traced here: 362 us
  waiting for transfers between devices  135 us (37%)
  blocking collectives  99.8 us (27%)
  other arithmetic  45.6 us (13%)
  matrix products  41 us (11%)
  between operations  16.3 us (4%)
  local copies, waits for them, and re-layouts  12.4 us (3%)
  starting transfers between devices  11.7 us (3%)
    psum x1, waiting for transfers between devices, per_device(): lax.psum((user_first_g, user_second_g, item_first_g, item_second_g, loss_...  96.8 us
    psum x1, blocking collectives, per_device(): lax.psum((user_first_g, user_second_g, item_first_g, item_second_g, loss_...  40.8 us
    all_to_all x1, waiting for transfers between devices, per_device(): lax.all_to_all(lax.all_to_all(fetched, 'dp', split_axis=0, concat_axis=0,...  29.1 us
    dot_general x6, matrix products, tower_pass(): jnp.dot(hidden_act, second_w, precision=highest, preferred_element_type=j...  19.6 us
    all_to_all x1, blocking collectives, per_device(): lax.all_to_all(fetched, 'dp', split_axis=0, concat_axis=0, tiled=True)  18.2 us
    scatter-add x1, other arithmetic, per_device(): grad_rows = jnp.zeros_like(id_table).at[asked_rows.reshape(-1)].add(sent_...  15.8 us
    all_gather x1, blocking collectives, per_device(): lax.all_gather(user_vec, 'dp', axis=0, tiled=True).astype(jnp.bfloat16)  11.5 us
    all_to_all x1, blocking collectives, per_device(): lax.all_to_all(lax.all_to_all(fetch_rows[0], 'dp', split_axis=0, concat_a...  10.3 us
  transfers between devices with their start and end apart: 5, of which 4 were waited for; matrix products, arithmetic and copies ran while one was open for 4% of the time, Pallas kernels for 0%

commit v1 on v0

--- a/solution.py
+++ b/solution.py
@@ -115,7 +115,8 @@
     new_table = id_table - learn_rate * grad_rows / (jnp.sqrt(new_state)[:, None] + epsilon)
     loss_part = jnp.sum(log_z - matching_pair_logit)
     summed = lax.psum(
-        (user_first_g, user_second_g, item_first_g, item_second_g, loss_part), ("dp", "shard")
+        lax.psum((user_first_g, user_second_g, item_first_g, item_second_g, loss_part), "shard"),
+        "dp",
     )
     shard_number = lax.axis_size("dp") * lax.axis_size("shard")
     return (

time: 363 us -> 314 us (0.87)
  waiting for transfers between devices: 135 us -> 105 us
  blocking collectives: 99.8 us -> 85.5 us
    psum x1, waiting for transfers between devices: 96.8 us -> 31.7 us  [per_device(): lax.psum((user_first_g, user_second_g, item_first_g, item_second_g, loss_...]
    psum x0 -> x1, waiting for transfers between devices: none -> 30.7 us  [per_device(): lax.psum(lax.psum((user_first_g, user_second_g, item_first_g, item_second...]
    psum x1, blocking collectives: 40.8 us -> 17.9 us  [per_device(): lax.psum((user_first_g, user_second_g, item_first_g, item_second_g, loss_...]
    psum x0 -> x1, blocking collectives: none -> 9.67 us  [per_device(): lax.psum(lax.psum((user_first_g, user_second_g, item_first_g, item_second...]
  transfers between devices with their start and end apart: 5 -> 6, of which waited for: 4 -> 5; matrix products, arithmetic and copies ran while one was open for 4% -> 13% of each run, Pallas kernels for 0% -> 0%
where the time goes in v1:
time: 314 us; the launch traced here: 313 us
  waiting for transfers between devices  105 us (33%)
  blocking collectives  85.5 us (27%)
  other arithmetic  43 us (14%)
  matrix products  37.5 us (12%)
  between operations  16 us (5%)
  local copies, waits for them, and re-layouts  13.7 us (4%)
  starting transfers between devices  12.7 us (4%)
    psum x1, waiting for transfers between devices, per_device(): lax.psum((user_first_g, user_second_g, item_first_g, item_second_g, loss_...  31.7 us
    psum x1, waiting for transfers between devices, per_device(): lax.psum(lax.psum((user_first_g, user_second_g, item_first_g, item_second...  30.7 us
    all_to_all x1, waiting for transfers between devices, per_device(): lax.all_to_all(lax.all_to_all(fetched, 'dp', split_axis=0, concat_axis=0,...  29.1 us
    dot_general x6, matrix products, tower_pass(): jnp.dot(hidden_act, second_w, precision=highest, preferred_element_type=j...  19.7 us
    all_to_all x1, blocking collectives, per_device(): lax.all_to_all(fetched, 'dp', split_axis=0, concat_axis=0, tiled=True)  18.2 us
    psum x1, blocking collectives, per_device(): lax.psum((user_first_g, user_second_g, item_first_g, item_second_g, loss_...  17.9 us
    scatter-add x1, other arithmetic, per_device(): grad_rows = jnp.zeros_like(id_table).at[asked_rows.reshape(-1)].add(sent_...  15.7 us
    all_gather x1, waiting for transfers between devices, per_device(): lax.all_gather(item_bf, 'dp', axis=0, tiled=True)  11.3 us
  transfers between devices with their start and end apart: 6, of which 5 were waited for; matrix products, arithmetic and copies ran while one was open for 13% of the time, Pallas kernels for 0%

profile of v1, /device:TPU:0, one launch (start us, length us, event | category | flops | bytes accessed | tf_op | source)
XLA Modules:
  0.0 313.3 jit_solution(8629353732001511194)
XLA Ops:
  7.2 10.0 %all_to_all.30 = s32[4,8,72]{2,1,0:T(8,128)S(1)} all-to-all(s32[4,8,72]{2,1,0:T(8,128)} %bitcast.32), channel_id=1, replica_groups=mesh['dp'=4,'shard'=8] {'dp'}, dimensions={0} | all-to-all | bytes 18432 | tf_op jit(solution)/shard_map/all_to_all | solution.py:49
  17.2 10.3 %all_to_all.31 = s32[4,8,72]{2,0,1:T(4,128)S(1)} all-to-all(s32[4,8,72]{2,0,1:T(4,128)S(1)} %copy.24), channel_id=1, replica_groups=mesh['dp'=4,'shard'=8] {'shard'}, dimensions={1} | all-to-all | bytes 18432 | tf_op jit(solution)/shard_map/all_to_all | solution.py:48
  27.7 6.1 %gather_fusion = f32[2304,128]{1,0:T(8,128)S(1)} fusion(f32[8192,128]{1,0:T(8,128)} %param.10, s32[3072]{0:T(1024)S(1)} %pad_clamp_fusion), kind=kCustom, calls=%fused_computation | custom fusion | bytes 2368512 | tf_op jit(solution)/shard_map/jit(_take)/gather | solution.py:55
  33.8 0.5 broadcast_select_fusion
  34.3 18.2 %all_to_all.32 = f32[4,8,72,128]{3,2,1,0:T(8,128)S(1)} all-to-all(f32[4,8,72,128]{3,2,1,0:T(8,128)S(1)} %broadcast_select_fusion), channel_id=1, replica_groups=mesh['dp'=4,'shard'=8] {'dp'}, dimensions={0} | all-to-all | bytes 2359296 | tf_op jit(solution)/shard_map/all_to_all | solution.py:59
  52.5 1.1 copy.27
  53.6 3.6 %all-to-all-start.3 = ((f32[4,8,72,128]{3,2,0,1:T(8,128)}), f32[4,8,72,128]{3,2,0,1:T(8,128)S(1)}, u32[]{:S(2)}, u32[]{:S(2)}) async-start(f32[4,8,72,128]{3,2,0,1:T(8,128)} %copy.27), calls=%async_computation.3 | async-start | bytes 2359296 | tf_op jit(solution)/shard_map/all_to_all | solution.py:58
  57.4 29.1 %all-to-all-done.3 = f32[4,8,72,128]{3,2,0,1:T(8,128)S(1)} async-done(((f32[4,8,72,128]{3,2,0,1:T(8,128)}), f32[4,8,72,128]{3,2,0,1:T(8,128)S(1)}, u32[]{:S(2)}, u32[]{:S(2)}) %all-to-all-start.3) | async-done | bytes 1179680 | tf_op jit(solution)/shard_map/all_to_all | solution.py:58
  86.6 2.6 gather_fusion.1
  89.2 0.3 broadcast_select_fusion.1
  89.5 1.8 fusion.30
  91.3 2.7 multiply_reduce_fusion.2
  94.1 0.9 divide_convert_fusion
  95.0 1.0 fusion.41
  96.0 2.6 multiply_reduce_fusion.4
  98.8 11.1 %all_gather.10 = bf16[2048,128]{0,1:T(8,128)(2,1)S(1)} all-gather(bf16[512,128]{0,1:T(8,128)(2,1)S(1)} %get-tuple-element.28), channel_id=1, replica_groups=mesh['dp'=4,'shard'=8] {'dp'}, dimensions={0}, use_global_device_ids=true | all-gather | bytes 655360 | tf_op jit(solution)/shard_map/all_gather | solution.py:82
  109.9 11.3 %all-gather.3.cloned.1.call-done = bf16[4096,128]{0,1:T(8,128)(2,1)} async-done(((bf16[1024,128]{0,1:T(8,128)(2,1)}), bf16[4096,128]{0,1:T(8,128)(2,1)}) %all-gather.3.cloned.1.call-update) | async-done | bytes 1048592 | tf_op jit(solution)/shard_map/all_gather | solution.py:78
  121.2 2.8 fusion
  124.0 0.6 subtract_reduce_fusion
  124.6 2.3 multiply_reduce_fusion.3
  126.9 8.2 %all-gather = f32[4,1,512]{2,1,0:T(1,128)S(1)} all-gather(f32[1,1,512]{2,1,0:T(1,128)S(1)} %bitcast.34), channel_id=1, replica_groups=mesh['dp'=4,'shard'=8] {'dp'}, dimensions={0}, use_global_device_ids=true | all-gather | bytes 10240 | tf_op jit(solution)/shard_map/all_gather | solution.py:83
  135.1 2.1 fusion.10
  137.4 0.7 copy-done.9
  138.1 4.4 %fusion.6 = f32[1024,512]{1,0:T(8,128)S(1)} fusion(f32[1024,512]{1,0:T(8,128)} %copy-done.6, f32[512,128]{1,0:T(8,128)S(1)} %copy-done, f32[1024,128]{0,1:T(8,128)} %copy-done.7, f32[1024,128]{0,1:T(8,128)} %copy-done.9, f32[1024]{0:T(1024)S(1)} %multiply_multiply_fusion, f32[1024]{0:T(1024)S(1)} %get-tuple-element.32), kind=kOutput, calls=%fused_computation.14 | convolution fusion | flops 810680320 | bytes 5513216 | tf_op jit(solution)/shard_map/transpose(jvp())/dot_general | solution.py:17
  142.5 2.6 fusion.58
  145.2 1.3 fusion.19
  146.5 1.0 copy-done.2
  147.4 1.7 fusion.57
  149.1 10.4 %scatter_custom_fusion = f32[2304,128]{1,0:T(8,128)} fusion(s32[1536]{0:T(1024)S(1)} %fusion.48, f32[1024,128]{1,0:T(8,128)} %fusion.58, f32[]{:T(128)} %constant.111, f32[512,128]{1,0:T(8,128)} %fusion.57, f32[]{:T(128)} %constant.90.clone.1), kind=kCustom, calls=%fused_computation.28 | custom fusion | flops 393216 | bytes 1966088 | tf_op jit(solution)/shard_map/scatter-add | solution.py:95
  159.5 2.2 convert_element_type.35
  161.6 4.4 %all-to-all-start.4 = ((bf16[4,8,72,128]{3,2,1,0:T(8,128)(2,1)}), bf16[4,8,72,128]{3,2,1,0:T(8,128)(2,1)}, u32[]{:S(2)}, u32[]{:S(2)}) async-start(bf16[4,8,72,128]{3,2,1,0:T(8,128)(2,1)} %bitcast.31), calls=%async_computation.4 | async-start | bytes 1179648 | tf_op jit(solution)/shard_map/all_to_all | solution.py:97
  166.0 2.1 fusion.28
  168.1 2.6 fusion.43
  170.8 2.1 all-to-all-done.4
  172.8 1.9 copy.29
  174.7 4.6 %all-to-all-start.5 = ((bf16[4,8,72,128]{3,2,0,1:T(8,128)(2,1)}), bf16[4,8,72,128]{3,2,0,1:T(8,128)(2,1)S(1)}, u32[]{:S(2)}, u32[]{:S(2)}) async-start(bf16[4,8,72,128]{3,2,0,1:T(8,128)(2,1)} %copy.29), calls=%async_computation.5 | async-start | bytes 1179648 | tf_op jit(solution)/shard_map/all_to_all | solution.py:96
  179.4 1.5 fusion.39
  180.9 6.0 %fusion.32 = f32[512,128]{1,0:T(8,128)} fusion(f32[1024,512]{1,0:T(8,128)} %copy-done.6, f32[1024,128]{0,1:T(8,128)S(1)} %copy-done.8, f32[1024,128]{0,1:T(8,128)} %copy-done.9, f32[1024]{0:T(1024)S(1)} %multiply_multiply_fusion, f32[1024]{0:T(1024)S(1)} %get-tuple-element.32), kind=kOutput, calls=%fused_computation.45 | convolution fusion | flops 808058880 | bytes 3416064 | tf_op jit(solution)/shard_map/transpose(jvp())/dot_general | solution.py:17
  187.0 17.9 %psum.78 = f32[]{:T(128)} all-reduce(f32[]{:T(128)} %get-tuple-element.33), channel_id=1, replica_groups=mesh['dp'=4,'shard'=8] {'shard'}, use_global_device_ids=true, to_apply=%region_18.19 | all-reduce | flops 1 | bytes 8 | tf_op jit(solution)/shard_map/psum | solution.py:118
  205.0 9.7 %psum.79 = f32[]{:T(128)} all-reduce(f32[]{:T(128)} %psum.78), channel_id=1, replica_groups=mesh['dp'=4,'shard'=8] {'dp'}, use_global_device_ids=true, to_apply=%region_19.20 | all-reduce | flops 1 | bytes 8 | tf_op jit(solution)/shard_map/psum | solution.py:117
  215.3 31.7 %all-reduce.5.cloned.1.call-done = (f32[128,512]{1,0:T(8,128)}, f32[512,128]{1,0:T(8,128)}, f32[128,512]{1,0:T(8,128)}, f32[512,128]{1,0:T(8,128)}) async-done(((f32[128,512]{1,0:T(8,128)}, f32[512,128]{1,0:T(8,128)}, f32[128,512]{1,0:T(8,128)}, f32[512,128]{1,0:T(8,128)}), (f32[128,512]{1,0:T(8,128)}, f32[512,128]{1,0:T(8,128)}, f32[128,512]{1,0:T(8,128)}, ...) | async-done | bytes 1048592 | tf_op jit(solution)/shard_map/psum | solution.py:118
  247.1 15.7 %scatter_custom_fusion.1 = f32[8192,128]{1,0:T(8,128)} fusion(s32[2304]{0:T(1024)S(1)} %fusion.47, f32[]{:T(128)} %constant.90.clone.1, bf16[2304,128]{1,0:T(8,128)(2,1)S(1)} %bitcast.30), kind=kCustom, calls=%fused_computation.17 | custom fusion | flops 589824 | bytes 4784132 | tf_op jit(solution)/shard_map/scatter-add | solution.py:112
  262.8 3.5 %multiply_reduce_fusion = f32[8192]{0:T(1024)S(1)} fusion(f32[8192,128]{1,0:T(8,128)} %scatter_custom_fusion.1), kind=kLoop, calls=%fused_computation.10 | loop fusion | flops 2088960 | bytes 4227072 | tf_op jit(solution)/shard_map/reduce_sum | solution.py:114
  266.3 0.6 sqrt_add_fusion
  267.0 4.3 %divide_subtract_fusion = f32[8192,128]{1,0:T(8,128)} fusion(f32[8192,128]{1,0:T(8,128)S(1)} %copy-done.1, f32[8192,128]{1,0:T(8,128)} %scatter_custom_fusion.1, f32[8192]{0:T(1024)S(1)} %get-tuple-element.29), kind=kLoop, calls=%fused_computation.9 | loop fusion | flops 3145728 | bytes 12615680 | tf_op jit(solution)/shard_map/sub | solution.py:115
  271.3 30.7 %all-reduce.7.cloned.1.call-done = (f32[128,512]{1,0:T(8,128)}, f32[512,128]{1,0:T(8,128)}, f32[128,512]{1,0:T(8,128)}, f32[512,128]{1,0:T(8,128)}) async-done(((f32[128,512]{1,0:T(8,128)}, f32[512,128]{1,0:T(8,128)}, f32[128,512]{1,0:T(8,128)}, f32[512,128]{1,0:T(8,128)}), (f32[128,512]{1,0:T(8,128)}, f32[512,128]{1,0:T(8,128)}, f32[128,512]{1,0:T(8,128)}, ...) | async-done | bytes 1048592 | tf_op jit(solution)/shard_map/psum | solution.py:117
  301.9 1.9 broadcast_multiply_fusion.2
  303.8 1.9 broadcast_multiply_fusion
  (69 shorter events, 0.9 us)
Async XLA Ops:
  7.2 84.1 %copy-start = (f32[512,128]{1,0:T(8,128)S(1)}, f32[512,128]{1,0:T(8,128)}, u32[]{:S(2)}) copy-start(f32[512,128]{1,0:T(8,128)} %param.15) | copy-start | bytes 786436
  52.5 4.7 %copy-start.20 = (s32[1,1536]{1,0:T(1,128)S(1)}, s32[1,1536]{1,0:T(1,128)}, u32[]{:S(2)}) copy-start(s32[1,1536]{1,0:T(1,128)} %param.17) | copy-start | bytes 18436
  53.6 32.9 %all-to-all-start.3 = ((f32[4,8,72,128]{3,2,0,1:T(8,128)}), f32[4,8,72,128]{3,2,0,1:T(8,128)S(1)}, u32[]{:S(2)}, u32[]{:S(2)}) async-start(f32[4,8,72,128]{3,2,0,1:T(8,128)} %copy.27), calls=%async_computation.3 | async-start | bytes 2359296 | tf_op jit(solution)/shard_map/all_to_all | solution.py:58
  57.2 64.0 %all-gather.3.cloned.1.call-start = ((), (), s32[]{:S(2)}) async-start(), calls=%async_computation.6 | async-start | bytes 1310720 | tf_op jit(solution)/shard_map/all_gather | solution.py:78
  86.6 2.9 copy-start.15
  91.3 2.8 copy-start.6
  91.3 3.7 %copy-start.13 = (f32[128,512]{1,0:T(8,128)S(1)}, f32[128,512]{1,0:T(8,128)}, u32[]{:S(2)}) copy-start(f32[128,512]{1,0:T(8,128)} %param.12) | copy-start | bytes 786436
  94.1 43.3 %copy-start.7 = (f32[1024,128]{0,1:T(8,128)}, f32[1024,128]{0,1:T(8,128)S(1)}, u32[]{:S(2)}) copy-start(f32[1024,128]{0,1:T(8,128)S(1)} %get-tuple-element.38) | copy-start | bytes 1572868
  96.0 2.7 copy-start.10
  96.0 2.7 copy-start.5
  121.2 3.4 %copy-start.4 = (bf16[4096,128]{0,1:T(8,128)(2,1)S(1)}, bf16[4096,128]{0,1:T(8,128)(2,1)}, u32[]{:S(2)}) copy-start(bf16[4096,128]{0,1:T(8,128)(2,1)} %all-gather.3.cloned.1.call-done) | copy-start | bytes 3145732
  137.3 0.8 copy-start.9
  138.1 4.4 %copy-start.16 = (f32[128,512]{1,0:T(8,128)S(1)}, f32[128,512]{1,0:T(8,128)}, u32[]{:S(2)}) copy-start(f32[128,512]{1,0:T(8,128)} %param.14) | copy-start | bytes 786436
  142.5 2.6 copy-start.11
  142.5 2.6 copy-start.17
  142.5 2.6 copy-start.21
  145.1 2.3 copy-start.14
  146.5 1.0 copy-start.2
  161.6 11.2 %all-to-all-start.4 = ((bf16[4,8,72,128]{3,2,1,0:T(8,128)(2,1)}), bf16[4,8,72,128]{3,2,1,0:T(8,128)(2,1)}, u32[]{:S(2)}, u32[]{:S(2)}) async-start(bf16[4,8,72,128]{3,2,1,0:T(8,128)(2,1)} %bitcast.31), calls=%async_computation.4 | async-start | bytes 1179648 | tf_op jit(solution)/shard_map/all_to_all | solution.py:97
  166.0 2.1 copy-start.12
  166.0 2.1 copy-start.18
  170.8 8.7 %copy-start.3 = (f32[512,512]{1,0:T(8,128)S(1)}, f32[512,512]{1,0:T(8,128)}, u32[]{:S(2)}) copy-start(f32[512,512]{1,0:T(8,128)} %copy-done.2) | copy-start | bytes 3145732
  170.8 10.1 %copy-start.8 = (f32[1024,128]{0,1:T(8,128)S(1)}, f32[1024,128]{0,1:T(8,128)}, u32[]{:S(2)}) copy-start(f32[1024,128]{0,1:T(8,128)} %copy-done.7) | copy-start | bytes 1572868
  174.7 72.3 %all-to-all-start.5 = ((bf16[4,8,72,128]{3,2,0,1:T(8,128)(2,1)}), bf16[4,8,72,128]{3,2,0,1:T(8,128)(2,1)S(1)}, u32[]{:S(2)}, u32[]{:S(2)}) async-start(bf16[4,8,72,128]{3,2,0,1:T(8,128)(2,1)} %copy.29), calls=%async_computation.5 | async-start | bytes 1179648 | tf_op jit(solution)/shard_map/all_to_all | solution.py:96
  179.4 67.6 %all-reduce.5.cloned.1.call-start = ((), (), s32[]{:S(2)}) async-start(), calls=%async_computation.7 | async-start | bytes 2097152 | tf_op jit(solution)/shard_map/psum | solution.py:118
  187.0 115.0 %all-reduce.7.cloned.1.call-start = ((), (), s32[]{:S(2)}) async-start(), calls=%async_computation.8 | async-start | bytes 2097152 | tf_op jit(solution)/shard_map/psum | solution.py:117
  262.8 3.5 %copy-start.19 = (f32[8192]{0:T(1024)S(1)}, f32[8192]{0:T(1024)}, u32[]{:S(2)}) copy-start(f32[8192]{0:T(1024)} %param.11) | copy-start | bytes 98308
  262.8 4.2 %copy-start.1 = (f32[8192,128]{1,0:T(8,128)S(1)}, f32[8192,128]{1,0:T(8,128)}, u32[]{:S(2)}) copy-start(f32[8192,128]{1,0:T(8,128)} %param.10) | copy-start | bytes 12582916
Sparse Core Ops, SparseCore 0:
  95.1 26.0 all-gather.2
  187.1 59.8 all-reduce.4
  250.2 51.6 all-reduce.6
